TPU v7x, 32 devices: a whole 2x2x4 slice. The times are simulated.
32 devices in a mesh: dp: 8 (over z, x), tensor: 4 (over y, core).
Axes of the slice: x: 2, y: 2, z: 4, core: 2. Of those that a mesh axis runs over, the one named last changes fastest.
Arguments:
- tokens: bfloat16 [16384, 1024], P(('dp', 'tensor')), may hold values from -6 to 6
- condition: bfloat16 [16, 1024], P('dp'), may hold values from -6 to 6
- ada_weight: bfloat16 [1024, 6144], P(None, 'tensor'), may hold values from -0.1875 to 0.1875
- ada_bias: bfloat16 [6144], P('tensor'), may hold values from -3 to 3
- qkv_weight: bfloat16 [1024, 3, 1024], P(None, None, 'tensor'), may hold values from -0.1875 to 0.1875
- qv_bias: bfloat16 [2, 1024], P(None, 'tensor'), may hold values from -3 to 3
- proj_weight: bfloat16 [1024, 1024], P('tensor'), may hold values from -0.75 to 0.75
- proj_bias: bfloat16 [1024], replicated, may hold values from -3 to 3
- up_weight: bfloat16 [4096, 1024], P('tensor'), may hold values from -0.1875 to 0.1875
- up_bias: bfloat16 [4096], P('tensor'), may hold values from -3 to 3
- down_weight: bfloat16 [4096, 1024], P('tensor'), may hold values from -0.09375 to 0.09375
- down_bias: bfloat16 [1024], replicated, may hold values from -3 to 3
- out_grad: bfloat16 [16384, 1024], P(('dp', 'tensor')), may hold values from -6 to 6
Outputs:
- block_out: bfloat16 [16384, 1024], P(('dp', 'tensor'))
- tokens_grad: float32 [16384, 1024], P(('dp', 'tensor'))
- condition_grad: float32 [16, 1024], P('dp')
- ada_weight_grad: float32 [1024, 6144], P(None, 'tensor')
- ada_bias_grad: float32 [6144], P('tensor')
- qkv_weight_grad: float32 [1024, 3, 1024], P(None, None, 'tensor')
- qv_bias_grad: float32 [2, 1024], P(None, 'tensor')
- proj_weight_grad: float32 [1024, 1024], P('tensor')
- proj_bias_grad: float32 [1024], replicated
- up_weight_grad: float32 [4096, 1024], P('tensor')
- up_bias_grad: float32 [4096], P('tensor')
- down_weight_grad: float32 [4096, 1024], P('tensor')
- down_bias_grad: float32 [1024], replicated
All inputs are finite; a program needn't handle non-finite values.
Results may differ from a plain program's by a relative error of at most 0.023.
The roundings to bfloat16 on the way count: a program that leaves them out, or rounds other values in their place, can miss the bound.
Values may be sent and summed in bfloat16 or wider, within the bound.
No kernel may reach another device: no remote copies, remote signals or barrier semaphores. Data moves between devices by JAX's collectives and lax.ppermute only.
A program may use at most 256 MiB of HBM per device.

v0:
```python
import math
import jax
import jax.numpy as jnp
from jax import lax
from jax.sharding import PartitionSpec as P

D = 1024
HD = 64
SEQ = 1024
norm_eps = 1e-06
highest = lax.Precision.HIGHEST


def layer_norm(values):
    row_mean = jnp.mean(values, axis=-1, keepdims=True)
    centered = values - row_mean
    inv_std = lax.rsqrt(jnp.mean(centered * centered, axis=-1, keepdims=True) + norm_eps)
    return (centered * inv_std, inv_std)


def norm_back(grad_normed, normed, inv_std):
    mean_grad = jnp.mean(grad_normed, axis=-1, keepdims=True)
    mean_cross = jnp.mean(grad_normed * normed, axis=-1, keepdims=True)
    return inv_std * (grad_normed - mean_grad - normed * mean_cross)


def gelu_tanh(values):
    return jax.nn.gelu(values, approximate=True)


def attend_query(inputs):
    query_rows, kv_rows = inputs
    key_rows = kv_rows[:, 0]
    value_rows = kv_rows[:, 1]
    score_scale = 1.0 / math.sqrt(HD)
    query_count = query_rows.shape[0]
    block_rows = min(512, query_count)
    out_parts = []
    lse_parts = []
    for start_row in range(0, query_count, block_rows):
        query_blk = query_rows[start_row : start_row + block_rows]
        scores = (
            jnp.einsum("qhd,khd->hqk", query_blk, key_rows, preferred_element_type=jnp.float32)
            * score_scale
        )
        row_max = jnp.max(scores, axis=-1, keepdims=True)
        exp_scores = jnp.exp(scores - row_max)
        row_total = jnp.sum(exp_scores, axis=-1, keepdims=True)
        probs_low = (exp_scores / row_total).astype(jnp.bfloat16)
        out_parts.append(
            jnp.einsum(
                "hqk,khd->qhd", probs_low, value_rows, preferred_element_type=jnp.float32
            ).astype(jnp.bfloat16)
        )
        lse_parts.append(row_max[..., 0] + jnp.log(row_total[..., 0]))
    return (jnp.concatenate(out_parts, axis=0), jnp.concatenate(lse_parts, axis=1))


def attend_query_back(inputs):
    query_rows, kv_rows, grad_rows, lse_rows = inputs
    key_rows = kv_rows[:, 0]
    value_rows = kv_rows[:, 1]
    score_scale = 1.0 / math.sqrt(HD)
    query_count = query_rows.shape[0]
    block_rows = min(512, query_count)
    key_grad = jnp.zeros(key_rows.shape, jnp.float32)
    value_grad = jnp.zeros(value_rows.shape, jnp.float32)
    query_parts = []
    for start_row in range(0, query_count, block_rows):
        query_blk = query_rows[start_row : start_row + block_rows]
        grad_blk = grad_rows[start_row : start_row + block_rows]
        scores = (
            jnp.einsum("qhd,khd->hqk", query_blk, key_rows, preferred_element_type=jnp.float32)
            * score_scale
        )
        probs = jnp.exp(scores - lse_rows[:, start_row : start_row + block_rows, None])
        probs_low = probs.astype(jnp.bfloat16)
        value_grad = value_grad + jnp.einsum(
            "hqk,qhd->khd", probs_low, grad_blk, preferred_element_type=jnp.float32
        )
        prob_grad = jnp.einsum(
            "qhd,khd->hqk", grad_blk, value_rows, preferred_element_type=jnp.float32
        )
        row_delta = jnp.sum(probs * prob_grad, axis=-1, keepdims=True)
        score_grad = (probs * (prob_grad - row_delta)).astype(jnp.bfloat16)
        query_parts.append(
            jnp.einsum("hqk,khd->qhd", score_grad, key_rows, preferred_element_type=jnp.float32)
            * score_scale
        )
        key_grad = (
            key_grad
            + jnp.einsum("hqk,qhd->khd", score_grad, query_blk, preferred_element_type=jnp.float32)
            * score_scale
        )
    query_grad = jnp.concatenate(query_parts, axis=0)
    return (query_grad, jnp.stack([key_grad, value_grad], axis=1))


def attend_latent(packed):
    out_rows, lse_rows = attend_query((packed[:, 0], packed[:, 1:]))
    return (out_rows, lse_rows)


def attend_back(inputs):
    packed, grad_lat, lse_lat = inputs
    query_grad, kv_grad = attend_query_back((packed[:, 0], packed[:, 1:], grad_lat, lse_lat))
    return jnp.concatenate([query_grad[:, None], kv_grad], axis=1).astype(jnp.bfloat16)


def shards(
    tokens,
    condition,
    ada_weight,
    ada_bias,
    qkv_weight,
    qv_bias,
    proj_weight,
    proj_bias,
    up_weight,
    up_bias,
    down_weight,
    down_bias,
    out_grad,
):
    rows_local = tokens.shape[0]
    latents_local = condition.shape[0]
    first_row = lax.axis_index("tensor") * rows_local
    row_latent = (first_row + jnp.arange(rows_local, dtype=jnp.int32)) // SEQ
    latent_pick = (
        row_latent[:, None] == jnp.arange(latents_local, dtype=jnp.int32)[None, :]
    ).astype(jnp.float32)
    cond_wide = condition.astype(jnp.float32)
    cond_sig = jax.nn.sigmoid(cond_wide)
    silu_low = (cond_wide * cond_sig).astype(jnp.bfloat16)
    mod_cols = (
        jnp.dot(silu_low, ada_weight, preferred_element_type=jnp.float32)
        + ada_bias.astype(jnp.float32)
    ).astype(jnp.bfloat16)
    mod_all = lax.all_gather(mod_cols, "tensor", axis=1, tiled=True).astype(jnp.float32)
    mod_rows = jnp.dot(latent_pick, mod_all, precision=highest)
    shift_attn, scale_attn, gate_attn, shift_mlp, scale_mlp, gate_mlp = [
        mod_rows[:, column_set * D : (column_set + 1) * D] for column_set in range(6)
    ]
    tokens_wide = tokens.astype(jnp.float32)
    normed_attn, inv_attn = layer_norm(tokens_wide)
    attn_input = (normed_attn * (1.0 + scale_attn) + shift_attn).astype(jnp.bfloat16)
    gathered_attn = lax.all_gather(attn_input, "tensor", axis=0, tiled=True)
    head_cols = qkv_weight.shape[2]
    heads_local = head_cols // HD
    qkv_flat = qkv_weight.reshape(D, 3 * head_cols)
    qkv_shift = jnp.concatenate([qv_bias[0], jnp.zeros_like(qv_bias[0]), qv_bias[1]]).astype(
        jnp.float32
    )
    qkv_rows = (
        jnp.dot(gathered_attn, qkv_flat, preferred_element_type=jnp.float32) + qkv_shift
    ).astype(jnp.bfloat16)
    latents_group = gathered_attn.shape[0] // SEQ
    qkv_packed = qkv_rows.reshape(latents_group, SEQ, 3, heads_local, HD)
    attn_heads, attn_lse = lax.map(attend_latent, qkv_packed)
    attn_flat = attn_heads.reshape(latents_group * SEQ, head_cols)
    proj_terms = jnp.dot(attn_flat, proj_weight, preferred_element_type=jnp.float32)
    branch_attn = lax.psum_scatter(
        proj_terms.astype(jnp.bfloat16), "tensor", scatter_dimension=0, tiled=True
    ).astype(jnp.float32) + proj_bias.astype(jnp.float32)
    hidden_state = tokens_wide + gate_attn * branch_attn
    normed_mlp, inv_mlp = layer_norm(hidden_state)
    mlp_input = (normed_mlp * (1.0 + scale_mlp) + shift_mlp).astype(jnp.bfloat16)
    gathered_mlp = lax.all_gather(mlp_input, "tensor", axis=0, tiled=True)
    pre_act = jnp.einsum(
        "rd,fd->rf", gathered_mlp, up_weight, preferred_element_type=jnp.float32
    ) + up_bias.astype(jnp.float32)
    hidden_low = gelu_tanh(pre_act).astype(jnp.bfloat16)
    down_terms = jnp.dot(hidden_low, down_weight, preferred_element_type=jnp.float32)
    branch_mlp = lax.psum_scatter(
        down_terms.astype(jnp.bfloat16), "tensor", scatter_dimension=0, tiled=True
    ).astype(jnp.float32) + down_bias.astype(jnp.float32)
    block_out = (hidden_state + gate_mlp * branch_mlp).astype(jnp.bfloat16)
    grad_wide = out_grad.astype(jnp.float32)
    grad_gate_mlp = grad_wide * branch_mlp
    grad_branch_mlp = (gate_mlp * grad_wide).astype(jnp.bfloat16)
    gathered_grad = lax.all_gather(grad_branch_mlp, "tensor", axis=0, tiled=True)
    grad_hidden = jnp.einsum(
        "rd,fd->rf", gathered_grad, down_weight, preferred_element_type=jnp.float32
    )
    grad_pre = jax.vjp(gelu_tanh, pre_act)[1](grad_hidden)[0].astype(jnp.bfloat16)
    down_weight_grad = jnp.einsum(
        "rf,rd->fd", hidden_low, gathered_grad, preferred_element_type=jnp.float32
    )
    up_weight_grad = jnp.einsum(
        "rf,rd->fd", grad_pre, gathered_mlp, preferred_element_type=jnp.float32
    )
    up_bias_grad = jnp.sum(grad_pre.astype(jnp.float32), axis=0)
    input_terms = jnp.dot(grad_pre, up_weight, preferred_element_type=jnp.float32)
    grad_mlp_input = lax.psum_scatter(
        input_terms.astype(jnp.bfloat16), "tensor", scatter_dimension=0, tiled=True
    ).astype(jnp.float32)
    grad_hidden_state = grad_wide + norm_back(
        grad_mlp_input * (1.0 + scale_mlp), normed_mlp, inv_mlp
    )
    grad_branch_attn = (gate_attn * grad_hidden_state).astype(jnp.bfloat16)
    gathered_back = lax.all_gather(grad_branch_attn, "tensor", axis=0, tiled=True)
    proj_weight_grad = jnp.einsum(
        "rc,rd->cd", attn_flat, gathered_back, preferred_element_type=jnp.float32
    )
    grad_attn_flat = jnp.einsum(
        "rd,cd->rc", gathered_back, proj_weight, preferred_element_type=jnp.float32
    ).astype(jnp.bfloat16)
    grad_heads = grad_attn_flat.reshape(latents_group, SEQ, heads_local, HD)
    grad_packed = lax.map(attend_back, (qkv_packed, grad_heads, attn_lse))
    grad_qkv = grad_packed.reshape(latents_group * SEQ, 3 * head_cols)
    qkv_weight_grad = jnp.einsum(
        "rd,rc->dc", gathered_attn, grad_qkv, preferred_element_type=jnp.float32
    ).reshape(qkv_weight.shape)
    bias_sums = jnp.sum(grad_qkv.astype(jnp.float32), axis=0).reshape(3, head_cols)
    qv_bias_grad = jnp.stack([bias_sums[0], bias_sums[2]])
    attn_terms = jnp.einsum("rc,dc->rd", grad_qkv, qkv_flat, preferred_element_type=jnp.float32)
    grad_attn_input = lax.psum_scatter(
        attn_terms.astype(jnp.bfloat16), "tensor", scatter_dimension=0, tiled=True
    ).astype(jnp.float32)
    tokens_grad = grad_hidden_state + norm_back(
        grad_attn_input * (1.0 + scale_attn), normed_attn, inv_attn
    )
    grad_mod_rows = jnp.concatenate(
        [
            grad_attn_input,
            grad_attn_input * normed_attn,
            grad_hidden_state * branch_attn,
            grad_mlp_input,
            grad_mlp_input * normed_mlp,
            grad_gate_mlp,
        ],
        axis=1,
    )
    grad_mod_local = jnp.dot(latent_pick.T, grad_mod_rows, precision=highest)
    grad_mod_cols = lax.psum_scatter(
        grad_mod_local.astype(jnp.bfloat16), "tensor", scatter_dimension=1, tiled=True
    )
    ada_weight_grad = jnp.dot(silu_low.T, grad_mod_cols, preferred_element_type=jnp.float32)
    ada_bias_grad = jnp.sum(grad_mod_cols.astype(jnp.float32), axis=0)
    silu_part = jnp.dot(grad_mod_cols, ada_weight.T, preferred_element_type=jnp.float32)
    proj_bias_part = jnp.sum(grad_branch_attn.astype(jnp.float32), axis=0)
    down_bias_part = jnp.sum(grad_branch_mlp.astype(jnp.float32), axis=0)
    silu_grad, proj_bias_grad, down_bias_grad = (
        lax.psum(silu_part.astype(jnp.bfloat16), "tensor").astype(jnp.float32),
        lax.psum(proj_bias_part.astype(jnp.bfloat16), "tensor").astype(jnp.float32),
        lax.psum(down_bias_part.astype(jnp.bfloat16), "tensor").astype(jnp.float32),
    )
    condition_grad = silu_grad * (cond_sig * (1.0 + cond_wide * (1.0 - cond_sig)))
    summed = (
        lax.psum(ada_weight_grad.astype(jnp.bfloat16), "dp").astype(jnp.float32),
        lax.psum(ada_bias_grad.astype(jnp.bfloat16), "dp").astype(jnp.float32),
        lax.psum(qkv_weight_grad.astype(jnp.bfloat16), "dp").astype(jnp.float32),
        lax.psum(qv_bias_grad.astype(jnp.bfloat16), "dp").astype(jnp.float32),
        lax.psum(proj_weight_grad.astype(jnp.bfloat16), "dp").astype(jnp.float32),
        lax.psum(proj_bias_grad.astype(jnp.bfloat16), "dp").astype(jnp.float32),
        lax.psum(up_weight_grad.astype(jnp.bfloat16), "dp").astype(jnp.float32),
        lax.psum(up_bias_grad.astype(jnp.bfloat16), "dp").astype(jnp.float32),
        lax.psum(down_weight_grad.astype(jnp.bfloat16), "dp").astype(jnp.float32),
        lax.psum(down_bias_grad.astype(jnp.bfloat16), "dp").astype(jnp.float32),
    )
    return (block_out, tokens_grad, condition_grad) + tuple(summed)


def solution(mesh):
    placed = (
        P(("dp", "tensor"), None),
        P("dp", None),
        P(None, "tensor"),
        P("tensor"),
        P(None, None, "tensor"),
        P(None, "tensor"),
        P("tensor", None),
        P(),
        P("tensor", None),
        P("tensor"),
        P("tensor", None),
        P(),
        P(("dp", "tensor"), None),
    )
    return jax.shard_map(
        shards,
        mesh=mesh,
        in_specs=placed,
        out_specs=(
            P(("dp", "tensor"), None),
            P(("dp", "tensor"), None),
            P("dp", None),
            P(None, "tensor"),
            P("tensor"),
            P(None, None, "tensor"),
            P(None, "tensor"),
            P("tensor", None),
            P(),
            P("tensor", None),
            P("tensor"),
            P("tensor", None),
            P(),
        ),
        check_vma=False,
    )
```

profile of v0, /device:TPU:0, one launch (start us, length us, event | category | flops | bytes accessed | tf_op | source)
XLA Modules:
  0.0 895.3 jit_solution(1262495356426923019)
XLA Ops:
  29.8 33.0 %all-gather.5.cloned.1.call-done = bf16[2048,1024]{1,0:T(8,128)(2,1)} async-done(((bf16[512,1024]{1,0:T(8,128)(2,1)}), bf16[2048,1024]{1,0:T(8,128)(2,1)}) %all-gather.5.cloned.1.call-update) | async-done | bytes 4194320 | tf_op jit(solution)/shard_map/all_gather | solution.py:147
  62.9 7.8 add_convert_fusion
  70.7 10.1 %reshape.206 = bf16[2,1024,3,4,64]{4,3,2,1,0:T(4,128)(2,1)} reshape(bf16[2048,768]{1,0:T(8,128)(2,1)} %add_convert_fusion) | data formatting | bytes 6291456 | tf_op jit(solution)/shard_map/reshape | solution.py:158
  80.8 9.8 %copy.41 = bf16[2,1024,3,4,64]{1,4,3,2,0:T(8,128)(2,1)} copy(bf16[2,1024,3,4,64]{4,3,2,1,0:T(4,128)(2,1)} %reshape.206) | data formatting | bytes 6291456 | tf_op jit(solution)/shard_map/while | solution.py:159
  90.7 27.7 %while.22 = (s32[]{:T(128)}, bf16[2,1024,4,64]{1,3,2,0:T(8,128)(2,1)}, f32[2,4,1024]{2,1,0:T(4,128)S(1)}, bf16[2,1024,3,4,64]{1,4,3,2,0:T(8,128)(2,1)}, s32[]{:T(128)}) while((s32[]{:T(128)}, bf16[2,1024,4,64]{1,3,2,0:T(8,128)(2,1)}, f32[2,4,1024]{2,1,0:T(4,128)S(1)}, bf16[2,1024,3,4,64]{1,4,3,2,0:T(8,128)(2,1)}, s32[]{:T(128)}) %tuple.75), condition=%wide.region_7.8_spmd, body=%wide.region_2.7_spmd.sunk | while | flops 1112801280 | bytes 66224264 | solution.py:159
  126.0 44.1 %reduce-scatter.8.cloned.1.call-done = bf16[512,1024]{1,0:T(8,128)(2,1)} async-done(((bf16[2048,1024]{1,0:T(8,128)(2,1)}), bf16[512,1024]{1,0:T(8,128)(2,1)}) %reduce-scatter.8.cloned.1.call-update) | async-done | bytes 1048592 | tf_op jit(solution)/shard_map/reduce_scatter | solution.py:162
  181.8 30.6 %all-gather.7.cloned.1.call-done = bf16[2048,1024]{1,0:T(8,128)(2,1)} async-done(((bf16[512,1024]{1,0:T(8,128)(2,1)}), bf16[2048,1024]{1,0:T(8,128)(2,1)}) %all-gather.7.cloned.1.call-update) | async-done | bytes 4194320 | tf_op jit(solution)/shard_map/all_gather | solution.py:168
  212.4 7.1 fusion.110
  223.5 6.9 convolution_convert_fusion.5
  230.5 18.4 %all-gather.9.cloned.1.call-done = bf16[2048,1024]{1,0:T(8,128)(2,1)} async-done(((bf16[512,1024]{1,0:T(8,128)(2,1)}), bf16[2048,1024]{1,0:T(8,128)(2,1)}) %all-gather.9.cloned.1.call-update) | async-done | bytes 4194320 | tf_op jit(solution)/shard_map/all_gather | solution.py:181
  248.9 14.5 %fusion.102 = (bf16[1024]{0:T(1024)(128)(2,1)}, bf16[2048,1024]{1,0:T(8,128)(2,1)S(1)}) fusion(f32[2048,1024]{1,0:T(8,128)} %copy-done.57, f32[1024]{0:T(1024)S(1)} %convert_element_type.208, bf16[2048,1024]{1,0:T(8,128)(2,1)} %all-gather.9.cloned.1.call-done, bf16[1024,1024]{1,0:T(8,128)(2,1)} %param.27), kind=kOutput, calls=%fused_computation.184 | convolution fusion | flops 4341103616 | bytes 18880512 | tf_op jit(solution)/shard_map/rd,fd->rf/dot_general | solution.py:182
  272.1 24.3 %reduce-scatter.10.cloned.1.call-done = bf16[512,1024]{1,0:T(8,128)(2,1)} async-done(((bf16[2048,1024]{1,0:T(8,128)(2,1)}), bf16[512,1024]{1,0:T(8,128)(2,1)}) %reduce-scatter.10.cloned.1.call-update) | async-done | bytes 1048592 | tf_op jit(solution)/shard_map/reduce_scatter | solution.py:174
  296.4 47.6 %reduce-scatter.12.cloned.1.call-done = bf16[512,1024]{1,0:T(8,128)(2,1)} async-done(((bf16[2048,1024]{1,0:T(8,128)(2,1)}), bf16[512,1024]{1,0:T(8,128)(2,1)}) %reduce-scatter.12.cloned.1.call-update) | async-done | bytes 1048592 | tf_op jit(solution)/shard_map/reduce_scatter | solution.py:194
  354.1 34.6 %all-gather.11.cloned.1.call-done = bf16[2048,1024]{1,0:T(8,128)(2,1)} async-done(((bf16[512,1024]{1,0:T(8,128)(2,1)}), bf16[2048,1024]{1,0:T(8,128)(2,1)}) %all-gather.11.cloned.1.call-update) | async-done | bytes 4194320 | tf_op jit(solution)/shard_map/all_gather | solution.py:201
  401.7 64.6 %while.23 = (s32[]{:T(128)}, bf16[2,1024,3,4,64]{1,4,3,2,0:T(8,128)(2,1)}, bf16[2,1024,3,4,64]{1,4,3,2,0:T(8,128)(2,1)}, f32[2,4,1024]{2,1,0:T(4,128)S(1)}, bf16...) while((s32[]{:T(128)}, bf16[2,1024,3,4,64]{1,4,3,2,0:T(8,128)(2,1)}, ...), condition=%wide.region_18.19_spmd, body=%wide.region_15.18_spmd.sunk | while | flops 2742284288 | bytes 173686992 | solution.py:209
  419.0 8.1 multiply_convert_fusion.8
  451.1 8.1 multiply_convert_fusion.8
  479.5 9.5 %convolution_convert_fusion.8 = bf16[1024,1024]{1,0:T(8,128)(2,1)} fusion(bf16[2048,1024]{1,0:T(8,128)(2,1)} %copy-done.56, bf16[2048,1024]{1,0:T(8,128)(2,1)} %all-gather.7.cloned.1.call-done), kind=kOutput, calls=%fused_computation.140 | convolution fusion | flops 4296015872 | bytes 10485760 | tf_op jit(solution)/shard_map/rf,rd->fd/dot_general | solution.py:189
  489.0 11.3 %convolution_convert_fusion.7 = bf16[1024,1024]{1,0:T(8,128)(2,1)} fusion(bf16[2048,1024]{1,0:T(8,128)(2,1)S(1)} %copy-done.53, f32[2048,1024]{1,0:T(8,128)} %copy-done.57, f32[1024]{0:T(1024)S(1)} %copy-done.47), kind=kOutput, calls=%fused_computation.139 | convolution fusion | flops 4316987392 | bytes 14684160 | tf_op jit(solution)/shard_map/rf,rd->fd/dot_general | solution.py:186
  505.4 18.6 %reduce-scatter.14.cloned.1.call-done = bf16[512,1024]{1,0:T(8,128)(2,1)} async-done(((bf16[2048,1024]{1,0:T(8,128)(2,1)}), bf16[512,1024]{1,0:T(8,128)(2,1)}) %reduce-scatter.14.cloned.1.call-update) | async-done | bytes 1048592 | tf_op jit(solution)/shard_map/reduce_scatter | solution.py:217
  546.0 23.3 %reduce-scatter.16.cloned.1.call-done = bf16[1536,2]{1,0:T(8,128)(2,1)} async-done(((bf16[6144,2]{1,0:T(8,128)(2,1)}), bf16[1536,2]{1,0:T(8,128)(2,1)}) %reduce-scatter.16.cloned.1.call-update) | async-done | bytes 6160
  580.3 6.8 all-reduce.2
  587.2 39.6 %all-reduce = (bf16[1536]{0:T(1024)(128)(2,1)S(1)}, bf16[2,256]{1,0:T(2,128)(2,1)S(1)}, bf16[1024]{0:T(1024)(128)(2,1)S(1)}, bf16[1024]{0:T(1024)(128)(2,1)S(1)}, bf16[1024]{0:T(1024)(128)(2,1)S(1)}) all-reduce(bf16[1536]{0:T(1024)(128)(2,1)S(1)} %bitcast_reduce_fusion, ...), channel_id=1, replica_groups=mesh['dp'=8,'tensor'=4] {'dp'}, use_global_device_ids=true, to_apply=%region_26.27 | all-reduce | flops 5120 | bytes 20480 | tf_op jit(solution)/shard_map/psum | solution.py:251
  631.2 241.9 %all-reduce.5.cloned.1.call-done = (bf16[1024,1536]{1,0:T(8,128)(2,1)}, bf16[1024,3,256]{2,0,1:T(8,128)(2,1)}, bf16[256,1024]{1,0:T(8,128)(2,1)}, bf16[1024,1024]{1,0:T(8,128)(2,1)}, bf16[1024,1024]{1,0:T(8,128)(2,1)}) async-done(((bf16[1024,1536]{1,0:T(8,128)(2,1)}, bf16[1024,3,256]{2,0,1:T(8,128)(2,1)}, bf16[256,1024]{1,0:T(8,128)(2,1)}, bf16[1024,1024]{1,0:T(8,128)(2,1)}, bf16[1024,1024]{1,0:T(8,128)(2,1)}), ...) | async-done | bytes 9437200 | tf_op jit(solution)/shard_map/psum | solution.py:250
  (266 shorter events, 223.1 us)
Async XLA Ops:
  7.2 55.7 %all-gather.5.cloned.1.call-start = ((), (), s32[]{:S(2)}) async-start(), calls=%async_computation.5 | async-start | bytes 5242880 | tf_op jit(solution)/shard_map/all_gather | solution.py:147
  7.3 11.4 %copy-start.29 = (s32[512]{0:T(512)}, s32[512]{0:T(512)S(1)}, u32[]{:S(2)}) copy-start(s32[512]{0:T(512)S(1)} %add_select_fusion) | copy-start | bytes 6148
  8.9 11.7 %copy-start.33 = (f32[512]{0:T(512)}, f32[512]{0:T(512)S(1)}, u32[]{:S(2)}) copy-start(f32[512]{0:T(512)S(1)} %broadcast_multiply_fusion.5) | copy-start | bytes 6148
  26.6 143.5 %reduce-scatter.8.cloned.1.call-start = ((), (), s32[]{:S(2)}) async-start(), calls=%async_computation.6 | async-start | bytes 5242880 | tf_op jit(solution)/shard_map/reduce_scatter | solution.py:162
  125.4 87.0 %all-gather.7.cloned.1.call-start = ((), (), s32[]{:S(2)}) async-start(), calls=%async_computation.7 | async-start | bytes 5242880 | tf_op jit(solution)/shard_map/all_gather | solution.py:168
  126.0 46.7 %copy-start.39 = (f32[1024]{0:T(1024)}, f32[1024]{0:T(1024)S(1)}, u32[]{:S(2)}) copy-start(f32[1024]{0:T(1024)S(1)} %convert_element_type.206) | copy-start | bytes 12292
  172.8 176.7 %copy-start.31 = (f32[512]{0:T(512)}, f32[512]{0:T(512)S(1)}, u32[]{:S(2)}) copy-start(f32[512]{0:T(512)S(1)} %broadcast_multiply_fusion.4) | copy-start | bytes 6148
  174.1 175.4 %copy-start.35 = (f32[512]{0:T(512)}, f32[512]{0:T(512)S(1)}, u32[]{:S(2)}) copy-start(f32[512]{0:T(512)S(1)} %add_rsqrt_fusion) | copy-start | bytes 6148
  177.8 71.1 %all-gather.9.cloned.1.call-start = ((), (), s32[]{:S(2)}) async-start(), calls=%async_computation.9 | async-start | bytes 5242880 | tf_op jit(solution)/shard_map/all_gather | solution.py:181
  181.7 114.8 %reduce-scatter.10.cloned.1.call-start = ((), (), s32[]{:S(2)}) async-start(), calls=%async_computation.8 | async-start | bytes 5242880 | tf_op jit(solution)/shard_map/reduce_scatter | solution.py:174
  181.7 67.1 %copy-start.46 = (f32[1024]{0:T(1024)}, f32[1024]{0:T(1024)S(1)}, u32[]{:S(2)}) copy-start(f32[1024]{0:T(1024)S(1)} %convert_element_type.208) | copy-start | bytes 12292
  230.5 113.6 %reduce-scatter.12.cloned.1.call-start = ((), (), s32[]{:S(2)}) async-start(), calls=%async_computation.10 | async-start | bytes 5242880 | tf_op jit(solution)/shard_map/reduce_scatter | solution.py:194
  248.9 16.6 %copy-start.55 = (bf16[1024,1024]{1,0:T(8,128)(2,1)S(1)}, bf16[1024,1024]{1,0:T(8,128)(2,1)}, u32[]{:S(2)}) copy-start(bf16[1024,1024]{1,0:T(8,128)(2,1)} %param.25) | copy-start | bytes 6291460
  271.5 117.2 %all-gather.11.cloned.1.call-start = ((), (), s32[]{:S(2)}) async-start(), calls=%async_computation.11 | async-start | bytes 5242880 | tf_op jit(solution)/shard_map/all_gather | solution.py:201
  272.1 77.3 %copy-start.37 = (f32[1024]{0:T(1024)}, f32[1024]{0:T(1024)S(1)}, u32[]{:S(2)}) copy-start(f32[1024]{0:T(1024)S(1)} %convert_element_type.212) | copy-start | bytes 12292
  354.0 169.9 %reduce-scatter.14.cloned.1.call-start = ((), (), s32[]{:S(2)}) async-start(), calls=%async_computation.12 | async-start | bytes 5242880 | tf_op jit(solution)/shard_map/reduce_scatter | solution.py:217
  479.2 90.1 %reduce-scatter.16.cloned.1.call-start = ((), (), s32[]{:S(2)}) async-start(), calls=%async_computation.13 | async-start | bytes 1966080
  489.0 11.3 %copy-start.21 = (bf16[96,8,2,1024]{3,1,2,0:T(8,128)(2,1)S(1)}, bf16[96,8,2,1024]{3,1,2,0:T(8,128)(2,1)}, u32[]{:S(2)}) copy-start(bf16[96,8,2,1024]{3,1,2,0:T(8,128)(2,1)} %copy-done.20) | copy-start | bytes 9437188
  489.0 11.3 %copy-start.52 = (bf16[2048,1024]{1,0:T(8,128)(2,1)S(1)}, bf16[2048,1024]{1,0:T(8,128)(2,1)}, u32[]{:S(2)}) copy-start(bf16[2048,1024]{1,0:T(8,128)(2,1)} %all-gather.5.cloned.1.call-done) | copy-start | bytes 12582916
  500.3 25.3 %copy-start.34 = (f32[512]{0:T(512)S(1)}, f32[512]{0:T(512)}, u32[]{:S(2)}) copy-start(f32[512]{0:T(512)} %copy-done.33) | copy-start | bytes 6148
  500.3 25.3 %copy-start.43 = (f32[512]{0:T(512)S(1)}, f32[512]{0:T(512)}, u32[]{:S(2)}) copy-start(f32[512]{0:T(512)} %copy-done.42) | copy-start | bytes 6148
  505.4 23.6 %copy-start.40 = (f32[1024]{0:T(1024)S(1)}, f32[1024]{0:T(1024)}, u32[]{:S(2)}) copy-start(f32[1024]{0:T(1024)} %copy-done.39) | copy-start | bytes 12292
  541.1 28.2 %copy-start.41 = (bf16[2,1024]{1,0:T(2,128)(2,1)S(1)}, bf16[2,1024]{1,0:T(2,128)(2,1)}, u32[]{:S(2)}) copy-start(bf16[2,1024]{1,0:T(2,128)(2,1)} %param.18) | copy-start | bytes 12292
  541.1 331.9 %all-reduce.5.cloned.1.call-start = ((), (), s32[]{:S(2)}) async-start(), calls=%async_computation.14 | async-start | bytes 18874368 | tf_op jit(solution)/shard_map/psum | solution.py:250
  (49 other events, 187.1 us)
Sparse Core Ops, SparseCore 0:
  26.7 36.1 all-gather.4
  125.5 44.5 reduce-scatter.7
  177.9 34.4 all-gather.6
  214.4 34.4 all-gather.8
  251.8 44.5 reduce-scatter.9
  299.4 44.5 reduce-scatter.11
  354.1 34.4 all-gather.10
  479.3 44.5 reduce-scatter.13
  541.2 28.0 reduce-scatter.15
  574.5 298.5 all-reduce.4
where the time goes:
time: 900 us; the launch traced here: 895 us
  waiting for transfers between devices  516 us (57%)
  matrix products  152 us (17%)
  other arithmetic  82.5 us (9%)
  local copies, waits for them, and re-layouts  73.8 us (8%)
  blocking collectives  52.7 us (6%)
  between operations  15 us (2%)
    psum x1, waiting for transfers between devices, shards(): lax.psum(ada_weight_grad.astype(jnp.bfloat16), 'dp').astype(jnp.float32)  242 us
    reduce_scatter x1, waiting for transfers between devices, shards(): lax.psum_scatter(input_terms.astype(jnp.bfloat16), 'tensor', scatter_dime...  47.6 us
    reduce_scatter x1, waiting for transfers between devices, shards(): lax.psum_scatter(proj_terms.astype(jnp.bfloat16), 'tensor', scatter_dimen...  44.1 us
    psum x1, blocking collectives, shards(): lax.psum(ada_bias_grad.astype(jnp.bfloat16), 'dp').astype(jnp.float32)  39.6 us
    all_gather x1, waiting for transfers between devices, shards(): lax.all_gather(grad_branch_attn, 'tensor', axis=0, tiled=True)  34.6 us
    all_gather x1, waiting for transfers between devices, shards(): gathered_attn = lax.all_gather(attn_input, 'tensor', axis=0, tiled=True)  33 us
    all_gather x1, waiting for transfers between devices, shards(): gathered_mlp = lax.all_gather(mlp_input, 'tensor', axis=0, tiled=True)  30.6 us
    reduce_scatter x1, waiting for transfers between devices, shards(): lax.psum_scatter(down_terms.astype(jnp.bfloat16), 'tensor', scatter_dimen...  24.3 us
  transfers between devices with their start and end apart: 10, of which 10 were waited for; matrix products, arithmetic and copies ran while one was open for 9% of the time, Pallas kernels for 0%

commit v1 on v0

--- a/solution.py
+++ b/solution.py
@@ -247,7 +247,9 @@
     )
     condition_grad = silu_grad * (cond_sig * (1.0 + cond_wide * (1.0 - cond_sig)))
     summed = (
-        lax.psum(ada_weight_grad.astype(jnp.bfloat16), "dp").astype(jnp.float32),
+        jnp.sum(lax.all_gather(ada_weight_grad.astype(jnp.bfloat16), "dp"), axis=0).astype(
+            jnp.float32
+        ),
         lax.psum(ada_bias_grad.astype(jnp.bfloat16), "dp").astype(jnp.float32),
         lax.psum(qkv_weight_grad.astype(jnp.bfloat16), "dp").astype(jnp.float32),
         lax.psum(qv_bias_grad.astype(jnp.bfloat16), "dp").astype(jnp.float32),

time: 900 us -> 1300 us (1.44)
  waiting for transfers between devices: 516 us -> 884 us
  blocking collectives: 52.7 us -> 72.1 us
  other arithmetic: 82.5 us -> 98.7 us
    all_gather x0 -> x1, waiting for transfers between devices: none -> 401 us  [shards(): lax.all_gather(ada_weight_grad.astype(jnp.bfloat16), 'dp')]
    psum x1, waiting for transfers between devices: 242 us -> 208 us  [shards(): lax.psum(qkv_weight_grad.astype(jnp.bfloat16), 'dp').astype(jnp.float32)]
    psum x1, blocking collectives: 39.6 us -> 58.4 us  [shards(): lax.psum(ada_bias_grad.astype(jnp.bfloat16), 'dp').astype(jnp.float32)]
    reduce_sum x0 -> x1, other arithmetic: none -> 15.5 us  [shards(): jnp.sum(lax.all_gather(ada_weight_grad.astype(jnp.bfloat16), 'dp'), axis=0)]
  transfers between devices with their start and end apart: 10 -> 11, of which waited for: 10 -> 11; matrix products, arithmetic and copies ran while one was open for 9% -> 7% of each run, Pallas kernels for 0% -> 0%
where the time goes in v1:
time: 1300 us
  waiting for transfers between devices  884 us (68%)
  matrix products  152 us (12%)
  other arithmetic  98.7 us (8%)
  blocking collectives  72.1 us (6%)
  local copies, waits for them, and re-layouts  70.8 us (5%)
  between operations  14.7 us (1%)
    all_gather x1, waiting for transfers between devices, shards(): lax.all_gather(ada_weight_grad.astype(jnp.bfloat16), 'dp')  401 us
    psum x1, waiting for transfers between devices, shards(): lax.psum(qkv_weight_grad.astype(jnp.bfloat16), 'dp').astype(jnp.float32)  208 us
    psum x1, blocking collectives, shards(): lax.psum(ada_bias_grad.astype(jnp.bfloat16), 'dp').astype(jnp.float32)  58.4 us
    reduce_scatter x1, waiting for transfers between devices, shards(): lax.psum_scatter(input_terms.astype(jnp.bfloat16), 'tensor', scatter_dime...  47.6 us
    reduce_scatter x1, waiting for transfers between devices, shards(): lax.psum_scatter(proj_terms.astype(jnp.bfloat16), 'tensor', scatter_dimen...  44.1 us
    all_gather x1, waiting for transfers between devices, shards(): lax.all_gather(grad_branch_attn, 'tensor', axis=0, tiled=True)  34.6 us
    all_gather x1, waiting for transfers between devices, shards(): gathered_attn = lax.all_gather(attn_input, 'tensor', axis=0, tiled=True)  33 us
    all_gather x1, waiting for transfers between devices, shards(): gathered_mlp = lax.all_gather(mlp_input, 'tensor', axis=0, tiled=True)  30.6 us
  transfers between devices with their start and end apart: 11, of which 11 were waited for; matrix products, arithmetic and copies ran while one was open for 7% of the time, Pallas kernels for 0%

profile of v1, /device:TPU:0, one launch (start us, length us, event | category | flops | bytes accessed | tf_op | source)
XLA Modules:
  0.0 1295.1 jit_solution(1730815581424835026)
XLA Ops:
  29.8 33.0 %all-gather.7.cloned.1.call-done = bf16[2048,1024]{1,0:T(8,128)(2,1)} async-done(((bf16[512,1024]{1,0:T(8,128)(2,1)}), bf16[2048,1024]{1,0:T(8,128)(2,1)}) %all-gather.7.cloned.1.call-update) | async-done | bytes 4194320 | tf_op jit(solution)/shard_map/all_gather | solution.py:147
  62.9 7.8 add_convert_fusion
  70.7 10.1 reshape.207
  80.8 9.8 copy.41
  90.7 27.7 %while.22 = (s32[]{:T(128)}, bf16[2,1024,4,64]{1,3,2,0:T(8,128)(2,1)}, f32[2,4,1024]{2,1,0:T(4,128)S(1)}, bf16[2,1024,3,4,64]{1,4,3,2,0:T(8,128)(2,1)}, s32[]{:T(128)}) while((s32[]{:T(128)}, bf16[2,1024,4,64]{1,3,2,0:T(8,128)(2,1)}, f32[2,4,1024]{2,1,0:T(4,128)S(1)}, bf16[2,1024,3,4,64]{1,4,3,2,0:T(8,128)(2,1)}, s32[]{:T(128)}) %tuple.75), condition=%wide.region_7.8_spmd, body=%wide.region_2.7_spmd.sunk | while | flops 1112801280 | bytes 66224264 | solution.py:159
  126.0 44.1 %reduce-scatter.8.cloned.1.call-done = bf16[512,1024]{1,0:T(8,128)(2,1)} async-done(((bf16[2048,1024]{1,0:T(8,128)(2,1)}), bf16[512,1024]{1,0:T(8,128)(2,1)}) %reduce-scatter.8.cloned.1.call-update) | async-done | bytes 1048592 | tf_op jit(solution)/shard_map/reduce_scatter | solution.py:162
  181.8 30.6 %all-gather.9.cloned.1.call-done = bf16[2048,1024]{1,0:T(8,128)(2,1)} async-done(((bf16[512,1024]{1,0:T(8,128)(2,1)}), bf16[2048,1024]{1,0:T(8,128)(2,1)}) %all-gather.9.cloned.1.call-update) | async-done | bytes 4194320 | tf_op jit(solution)/shard_map/all_gather | solution.py:168
  230.5 18.4 %all-gather.11.cloned.1.call-done = bf16[2048,1024]{1,0:T(8,128)(2,1)} async-done(((bf16[512,1024]{1,0:T(8,128)(2,1)}), bf16[2048,1024]{1,0:T(8,128)(2,1)}) %all-gather.11.cloned.1.call-update) | async-done | bytes 4194320 | tf_op jit(solution)/shard_map/all_gather | solution.py:181
  248.9 14.5 %fusion.102 = (bf16[1024]{0:T(1024)(128)(2,1)}, bf16[2048,1024]{1,0:T(8,128)(2,1)S(1)}) fusion(f32[2048,1024]{1,0:T(8,128)} %copy-done.56, f32[1024]{0:T(1024)S(1)} %convert_element_type.210, bf16[2048,1024]{1,0:T(8,128)(2,1)} %all-gather.11.cloned.1.call-done, bf16[1024,1024]{1,0:T(8,128)(2,1)} %param.27), kind=kOutput, calls=%fused_computation.184 | convolution fusion | flops 4341103616 | bytes 18880512 | tf_op jit(solution)/shard_map/rd,fd->rf/dot_general | solution.py:182
  272.1 24.3 %reduce-scatter.10.cloned.1.call-done = bf16[512,1024]{1,0:T(8,128)(2,1)} async-done(((bf16[2048,1024]{1,0:T(8,128)(2,1)}), bf16[512,1024]{1,0:T(8,128)(2,1)}) %reduce-scatter.10.cloned.1.call-update) | async-done | bytes 1048592 | tf_op jit(solution)/shard_map/reduce_scatter | solution.py:174
  296.4 47.6 %reduce-scatter.12.cloned.1.call-done = bf16[512,1024]{1,0:T(8,128)(2,1)} async-done(((bf16[2048,1024]{1,0:T(8,128)(2,1)}), bf16[512,1024]{1,0:T(8,128)(2,1)}) %reduce-scatter.12.cloned.1.call-update) | async-done | bytes 1048592 | tf_op jit(solution)/shard_map/reduce_scatter | solution.py:194
  354.0 34.6 %all-gather.13.cloned.1.call-done = bf16[2048,1024]{1,0:T(8,128)(2,1)} async-done(((bf16[512,1024]{1,0:T(8,128)(2,1)}), bf16[2048,1024]{1,0:T(8,128)(2,1)}) %all-gather.13.cloned.1.call-update) | async-done | bytes 4194320 | tf_op jit(solution)/shard_map/all_gather | solution.py:201
  401.6 64.6 %while.23 = (s32[]{:T(128)}, bf16[2,1024,3,4,64]{1,4,3,2,0:T(8,128)(2,1)}, bf16[2,1024,3,4,64]{1,4,3,2,0:T(8,128)(2,1)}, f32[2,4,1024]{2,1,0:T(4,128)S(1)}, bf16...) while((s32[]{:T(128)}, bf16[2,1024,3,4,64]{1,4,3,2,0:T(8,128)(2,1)}, ...), condition=%wide.region_18.19_spmd, body=%wide.region_15.18_spmd.sunk | while | flops 2742284288 | bytes 173686992 | solution.py:209
  419.0 8.1 multiply_convert_fusion.8
  451.0 8.1 multiply_convert_fusion.8
  479.4 9.6 convolution_convert_fusion.8
  489.0 11.3 convolution_convert_fusion.7
  505.3 18.5 %reduce-scatter.14.cloned.1.call-done = bf16[512,1024]{1,0:T(8,128)(2,1)} async-done(((bf16[2048,1024]{1,0:T(8,128)(2,1)}), bf16[512,1024]{1,0:T(8,128)(2,1)}) %reduce-scatter.14.cloned.1.call-update) | async-done | bytes 1048592 | tf_op jit(solution)/shard_map/reduce_scatter | solution.py:217
  546.0 23.2 %reduce-scatter.16.cloned.1.call-done = bf16[1536,2]{1,0:T(8,128)(2,1)} async-done(((bf16[6144,2]{1,0:T(8,128)(2,1)}), bf16[1536,2]{1,0:T(8,128)(2,1)}) %reduce-scatter.16.cloned.1.call-update) | async-done | bytes 6160
  576.1 208.4 %all-reduce.5.cloned.1.call-done = (bf16[1024,3,256]{2,0,1:T(8,128)(2,1)}, bf16[256,1024]{1,0:T(8,128)(2,1)}, bf16[1024,1024]{1,0:T(8,128)(2,1)}, bf16[1024,1024]{1,0:T(8,128)(2,1)}) async-done(((bf16[1024,3,256]{2,0,1:T(8,128)(2,1)}, bf16[256,1024]{1,0:T(8,128)(2,1)}, bf16[1024,1024]{1,0:T(8,128)(2,1)}, bf16[1024,1024]{1,0:T(8,128)(2,1)}), (bf16[1024,3,256]{2,0,1:T(8,128)(2,1)}, ...) | async-done | bytes 6291472 | tf_op jit(solution)/shard_map/psum | solution.py:254
  796.0 7.3 all-reduce.2
  803.5 58.4 %all-reduce = (bf16[1536]{0:T(1024)(128)(2,1)S(1)}, bf16[2,256]{1,0:T(2,128)(2,1)S(1)}, bf16[1024]{0:T(1024)(128)(2,1)S(1)}, bf16[1024]{0:T(1024)(128)(2,1)S(1)}, bf16[1024]{0:T(1024)(128)(2,1)S(1)}) all-reduce(bf16[1536]{0:T(1024)(128)(2,1)S(1)} %bitcast_reduce_fusion, ...), channel_id=1, replica_groups=mesh['dp'=8,'tensor'=4] {'dp'}, use_global_device_ids=true, to_apply=%region_26.27 | all-reduce | flops 5120 | bytes 20480 | tf_op jit(solution)/shard_map/psum | solution.py:253
  866.2 401.0 %all-gather.15.cloned.1.call-done = bf16[8192,1536]{1,0:T(8,128)(2,1)} async-done(((bf16[1024,1536]{1,0:T(8,128)(2,1)}), bf16[8192,1536]{1,0:T(8,128)(2,1)}) %all-gather.15.cloned.1.call-update) | async-done | bytes 25165840 | tf_op jit(solution)/shard_map/all_gather | solution.py:250
  1267.3 15.5 %reduce_sum.185 = bf16[1024,1536]{1,0:T(8,128)(2,1)} reduce(bf16[8,1024,1536]{2,1,0:T(8,128)(2,1)} %bitcast.217, bf16[]{:T(256)} %constant.87.clone.1), dimensions={0}, to_apply=%region_24.25 | reduce | flops 11010048 | bytes 28311554 | tf_op jit(solution)/shard_map/reduce_sum | solution.py:250
  (268 shorter events, 235.0 us)
Async XLA Ops:
  7.2 55.7 %all-gather.7.cloned.1.call-start = ((), (), s32[]{:S(2)}) async-start(), calls=%async_computation.5 | async-start | bytes 5242880 | tf_op jit(solution)/shard_map/all_gather | solution.py:147
  7.3 11.4 copy-start.28
  8.9 11.7 copy-start.32
  26.6 143.5 %reduce-scatter.8.cloned.1.call-start = ((), (), s32[]{:S(2)}) async-start(), calls=%async_computation.6 | async-start | bytes 5242880 | tf_op jit(solution)/shard_map/reduce_scatter | solution.py:162
  125.4 87.0 %all-gather.9.cloned.1.call-start = ((), (), s32[]{:S(2)}) async-start(), calls=%async_computation.7 | async-start | bytes 5242880 | tf_op jit(solution)/shard_map/all_gather | solution.py:168
  126.0 46.7 %copy-start.38 = (f32[1024]{0:T(1024)}, f32[1024]{0:T(1024)S(1)}, u32[]{:S(2)}) copy-start(f32[1024]{0:T(1024)S(1)} %convert_element_type.208) | copy-start | bytes 12292
  172.8 176.6 %copy-start.30 = (f32[512]{0:T(512)}, f32[512]{0:T(512)S(1)}, u32[]{:S(2)}) copy-start(f32[512]{0:T(512)S(1)} %broadcast_multiply_fusion.4) | copy-start | bytes 6148
  174.1 175.3 %copy-start.34 = (f32[512]{0:T(512)}, f32[512]{0:T(512)S(1)}, u32[]{:S(2)}) copy-start(f32[512]{0:T(512)S(1)} %add_rsqrt_fusion) | copy-start | bytes 6148
  177.8 71.1 %all-gather.11.cloned.1.call-start = ((), (), s32[]{:S(2)}) async-start(), calls=%async_computation.9 | async-start | bytes 5242880 | tf_op jit(solution)/shard_map/all_gather | solution.py:181
  181.7 114.7 %reduce-scatter.10.cloned.1.call-start = ((), (), s32[]{:S(2)}) async-start(), calls=%async_computation.8 | async-start | bytes 5242880 | tf_op jit(solution)/shard_map/reduce_scatter | solution.py:174
  181.8 67.1 %copy-start.45 = (f32[1024]{0:T(1024)}, f32[1024]{0:T(1024)S(1)}, u32[]{:S(2)}) copy-start(f32[1024]{0:T(1024)S(1)} %convert_element_type.210) | copy-start | bytes 12292
  230.5 113.5 %reduce-scatter.12.cloned.1.call-start = ((), (), s32[]{:S(2)}) async-start(), calls=%async_computation.10 | async-start | bytes 5242880 | tf_op jit(solution)/shard_map/reduce_scatter | solution.py:194
  248.9 16.6 %copy-start.54 = (bf16[1024,1024]{1,0:T(8,128)(2,1)S(1)}, bf16[1024,1024]{1,0:T(8,128)(2,1)}, u32[]{:S(2)}) copy-start(bf16[1024,1024]{1,0:T(8,128)(2,1)} %param.25) | copy-start | bytes 6291460
  271.4 117.2 %all-gather.13.cloned.1.call-start = ((), (), s32[]{:S(2)}) async-start(), calls=%async_computation.11 | async-start | bytes 5242880 | tf_op jit(solution)/shard_map/all_gather | solution.py:201
  272.1 77.3 %copy-start.36 = (f32[1024]{0:T(1024)}, f32[1024]{0:T(1024)S(1)}, u32[]{:S(2)}) copy-start(f32[1024]{0:T(1024)S(1)} %convert_element_type.214) | copy-start | bytes 12292
  354.0 169.9 %reduce-scatter.14.cloned.1.call-start = ((), (), s32[]{:S(2)}) async-start(), calls=%async_computation.12 | async-start | bytes 5242880 | tf_op jit(solution)/shard_map/reduce_scatter | solution.py:217
  479.2 90.1 %reduce-scatter.16.cloned.1.call-start = ((), (), s32[]{:S(2)}) async-start(), calls=%async_computation.14 | async-start | bytes 1966080
  489.0 11.3 copy-start.21
  500.3 25.2 %copy-start.33 = (f32[512]{0:T(512)S(1)}, f32[512]{0:T(512)}, u32[]{:S(2)}) copy-start(f32[512]{0:T(512)} %copy-done.32) | copy-start | bytes 6148
  500.3 25.2 %copy-start.42 = (f32[512]{0:T(512)S(1)}, f32[512]{0:T(512)}, u32[]{:S(2)}) copy-start(f32[512]{0:T(512)} %copy-done.41) | copy-start | bytes 6148
  505.3 23.6 %copy-start.39 = (f32[1024]{0:T(1024)S(1)}, f32[1024]{0:T(1024)}, u32[]{:S(2)}) copy-start(f32[1024]{0:T(1024)} %copy-done.38) | copy-start | bytes 12292
  541.1 243.4 %all-reduce.5.cloned.1.call-start = ((), (), s32[]{:S(2)}) async-start(), calls=%async_computation.15 | async-start | bytes 12582912 | tf_op jit(solution)/shard_map/psum | solution.py:254
  545.7 23.5 %copy-start.40 = (bf16[2,1024]{1,0:T(2,128)(2,1)S(1)}, bf16[2,1024]{1,0:T(2,128)(2,1)}, u32[]{:S(2)}) copy-start(bf16[2,1024]{1,0:T(2,128)(2,1)} %param.18) | copy-start | bytes 12292
  545.7 721.6 %all-gather.15.cloned.1.call-start = ((), (), s32[]{:S(2)}) async-start(), calls=%async_computation.13 | async-start | bytes 28311552 | tf_op jit(solution)/shard_map/all_gather | solution.py:250
  (49 other events, 184.0 us)
Sparse Core Ops, SparseCore 0:
  26.7 36.1 all-gather.6
  125.5 44.5 reduce-scatter.7
  177.9 34.4 all-gather.8
  214.4 34.4 all-gather.10
  251.8 44.5 reduce-scatter.9
  299.4 44.5 reduce-scatter.11
  354.1 34.4 all-gather.12
  479.3 44.5 reduce-scatter.13
  541.2 27.9 reduce-scatter.15
  574.1 210.3 all-reduce.4
  786.6 480.6 all-gather.14
